TPU v7x, 32 devices: a whole 2x2x4 slice. The times are simulated.
32 devices in a mesh: freq: 4 (over z), tm: 4 (over x, core), grp: 2 (over y).
Axes of the slice: x: 2, y: 2, z: 4, core: 2. Of those that a mesh axis runs over, the one named last changes fastest.
Arguments:
- voltages: bfloat16 [4, 2, 1024, 4096], P(None, None, ('freq', 'grp'), 'tm'), may hold values from -6 to 6
- prior_gains: float32 [4, 2, 1024], P('freq'), may hold values from -4.2 to 4.2
- station_flags: int32 [512], replicated, may hold values 0 or 1
- ingest_map: int32 [512], replicated, may hold values from 0 to 511, each once
- station_coords: float32 [2, 512], replicated, may hold values from -40 to 40
- pointing: int32 [2, 256], replicated, may hold values from 0 to 63
- corr_channels: int32 [4], replicated, may hold values from 0 to 3, each once
- beam_channels: int32 [4], replicated, may hold values from 0 to 3, each once
Outputs:
- visibilities: float32 [4, 2, 1024, 1024], P('freq', None, 'grp', 'tm')
- solved_gains: float32 [4, 2, 1024], P('freq')
- tied_beams: bfloat16 [4, 2, 2, 256, 4096], P('freq', None, None, 'grp', 'tm')
Inputs may be any that keep to these rules, and one draw needn't show every extreme that they name: `ingest_map`: each station appears in exactly one ingest slot. `corr_channels`: each channel is handled by exactly one correlator slot. `beam_channels`: each channel is handled by exactly one beamformer slot.
All inputs are finite; a program needn't handle non-finite values.
Results may differ from a plain program's by a relative error of at most 0.0049.
Values may be sent and summed in bfloat16 or wider, within the bound.
A program may use at most 64 MiB of HBM per device.

v0:
```python
import math
import jax
import jax.numpy as jnp
from jax import lax
from jax.sharding import PartitionSpec as P

S = 512
ITERS = 4
grid_cells = 64.0


def weights_for(gains_sel, ratio, pointing_part, slot_coords):
    east_dir = (pointing_part[0].astype(jnp.float32) + 0.5) / grid_cells - 0.5
    north_dir = (pointing_part[1].astype(jnp.float32) + 0.5) / grid_cells - 0.5
    phase = (
        2.0
        * math.pi
        * ratio
        * (
            east_dir[:, None] * slot_coords[0][None, :]
            + north_dir[:, None] * slot_coords[1][None, :]
        )
    )
    cosine = jnp.cos(phase)
    sine = jnp.sin(phase)
    gain_real = gains_sel[0].reshape(2, S)
    gain_imag = gains_sel[1].reshape(2, S)
    denom = jnp.maximum(gain_real * gain_real + gain_imag * gain_imag, 0.5)
    along_real = gain_real / denom
    along_imag = gain_imag / denom
    factor = 1.0 / math.sqrt(S)
    w_real = (cosine[None] * along_real[:, None, :] - sine[None] * along_imag[:, None, :]) * factor
    w_imag = -(cosine[None] * along_imag[:, None, :] + sine[None] * along_real[:, None, :]) * factor
    upper = jnp.stack([w_real, -w_imag], axis=2)
    lower = jnp.stack([w_imag, w_real], axis=2)
    return jnp.stack([upper, lower], axis=1).astype(jnp.bfloat16)


def body(
    voltages,
    prior_gains,
    station_flags,
    ingest_map,
    station_coords,
    pointing,
    corr_channels,
    beam_channels,
):
    highest = lax.Precision.HIGHEST
    n_freq = lax.axis_size("freq")
    n_time = lax.axis_size("tm")
    n_group = lax.axis_size("grp")
    freq_index = lax.axis_index("freq")
    time_index = lax.axis_index("tm")
    group_index = lax.axis_index("grp")
    channels_all = voltages.shape[0]
    per_device = channels_all // n_freq
    per_input = voltages.shape[2]
    samples = voltages.shape[3]
    inputs_all = 2 * S
    corr_source = jnp.take(voltages, corr_channels, axis=0)
    beam_source = jnp.take(voltages, beam_channels, axis=0)
    corr_half, beam_half = (
        lax.all_to_all(corr_source, "freq", split_axis=0, concat_axis=2, tiled=True),
        lax.all_to_all(beam_source, "freq", split_axis=0, concat_axis=2, tiled=True),
    )
    split_shape = (per_device, 2, n_freq, per_input, samples)
    corr_pair, beam_pair = (
        lax.all_gather(corr_half.reshape(split_shape), "grp", axis=3, tiled=True),
        lax.all_gather(beam_half.reshape(split_shape), "grp", axis=3, tiled=True),
    )
    full_shape = (per_device, 2, inputs_all, samples)
    corr_volts = corr_pair.reshape(full_shape)
    beam_volts = beam_pair.reshape(full_shape)
    slot_keep = 1 - jnp.take(station_flags, ingest_map)
    keep = jnp.concatenate([slot_keep, slot_keep]).astype(jnp.bfloat16)
    corr_volts = corr_volts * keep[None, None, :, None]
    beam_volts = beam_volts * keep[None, None, :, None]
    rows = inputs_all // n_group
    row_start = group_index * rows
    mine = lax.dynamic_slice_in_dim(corr_volts, row_start, rows, 2)
    left = jnp.stack([mine, jnp.stack([mine[:, 1], -mine[:, 0]], axis=1)], axis=1)
    partial_value = jnp.einsum(
        "corit,crjt->coij", left, corr_volts, preferred_element_type=jnp.float32
    )
    partial_value = partial_value * (1.0 / (samples * n_time))
    columns = inputs_all // n_time
    vis_block = lax.psum_scatter(partial_value, "tm", scatter_dimension=3, tiled=True)
    gains = prior_gains
    for iteration in range(ITERS):
        power = jnp.sum(gains * gains, axis=(1, 2)) + 1e-06
        along = lax.dynamic_slice_in_dim(gains, time_index * columns, columns, 2)
        real_real = jnp.einsum("cij,cj->ci", vis_block[:, 0], along[:, 0], precision=highest)
        imag_imag = jnp.einsum("cij,cj->ci", vis_block[:, 1], along[:, 1], precision=highest)
        real_imag = jnp.einsum("cij,cj->ci", vis_block[:, 0], along[:, 1], precision=highest)
        imag_real = jnp.einsum("cij,cj->ci", vis_block[:, 1], along[:, 0], precision=highest)
        update = jnp.stack([real_real - imag_imag, imag_real + real_imag], axis=1)
        update = lax.psum(update, "tm")
        own_rows = lax.dynamic_slice_in_dim(gains, row_start, rows, 2)
        fresh = 0.5 * (own_rows + inputs_all * update / power[:, None, None])
        gains = lax.all_gather(fresh, "grp", axis=2, tiled=True)
    all_gains = lax.all_gather(gains, "freq", axis=0, tiled=True)
    my_beam = lax.dynamic_slice_in_dim(beam_channels, freq_index * per_device, per_device, 0)
    onehot = (corr_channels[None, :] == my_beam[:, None]).astype(jnp.float32)
    selected = jnp.einsum("ck,kri->cri", onehot, all_gains, precision=highest)
    ratio = 0.875 + 0.25 * (my_beam.astype(jnp.float32) + 0.5) / channels_all
    beams_mine = pointing.shape[1] // n_group
    pointing_part = lax.dynamic_slice_in_dim(pointing, group_index * beams_mine, beams_mine, 1)
    slot_coords = jnp.take(station_coords, ingest_map, axis=1)
    weights = jax.vmap(weights_for, in_axes=(0, 0, None, None))(
        selected, ratio, pointing_part, slot_coords
    )
    block = beam_volts.reshape(per_device, 2, 2, S, samples)
    beams = jnp.einsum("cpobrq,crpqt->cpobt", weights, block, preferred_element_type=jnp.float32)
    return (vis_block, gains, beams.astype(jnp.bfloat16))


def solution(mesh):
    return jax.shard_map(
        body,
        mesh=mesh,
        in_specs=(
            P(None, None, ("freq", "grp"), "tm"),
            P("freq", None, None),
            P(),
            P(),
            P(),
            P(),
            P(),
            P(),
        ),
        out_specs=(
            P("freq", None, "grp", "tm"),
            P("freq", None, None),
            P("freq", None, None, "grp", "tm"),
        ),
        check_vma=False,
    )
```

profile of v0, /device:TPU:0, one launch (start us, length us, event | category | flops | bytes accessed | tf_op | source)
XLA Modules:
  0.0 313.8 jit_solution(3851320219780948037)
XLA Ops:
  8.8 2.0 gather_fusion.2
  10.8 1.9 broadcast_select_fusion.1
  12.7 54.4 %all_to_all.30 = bf16[4,2,128,1024]{3,2,1,0:T(8,128)(2,1)} all-to-all(bf16[4,2,128,1024]{3,2,1,0:T(8,128)(2,1)S(1)} %broadcast_select_fusion.1), channel_id=1, replica_groups=mesh['freq'=4,'tm'=4,'grp'=2] {'freq'}, dimensions={0} | all-to-all | bytes 4194304 | tf_op jit(solution)/shard_map/all_to_all | solution.py:64
  67.2 2.0 gather_fusion.3
  69.2 1.9 broadcast_select_fusion
  71.1 50.7 %all_to_all.31 = bf16[4,2,128,1024]{3,2,1,0:T(8,128)(2,1)} all-to-all(bf16[4,2,128,1024]{3,2,1,0:T(8,128)(2,1)S(1)} %broadcast_select_fusion), channel_id=1, replica_groups=mesh['freq'=4,'tm'=4,'grp'=2] {'freq'}, dimensions={0} | all-to-all | bytes 4194304 | tf_op jit(solution)/shard_map/all_to_all | solution.py:65
  122.5 3.5 %gather_fusion = s32[512]{0:T(512)S(1)} fusion(s32[512]{0:T(512)S(1)} %copy-done.1, s32[1024]{0:T(1024)S(1)} %pad_clamp_fusion.1), kind=kCustom, calls=%fused_computation.2 | custom fusion | bytes 6144 | tf_op jit(solution)/shard_map/jit(_take)/gather | solution.py:75
  126.1 2.5 broadcast_multiply_fusion
  129.1 1.8 copy-done.3
  132.6 6.1 %fusion.5 = f32[1,2,512,1024]{3,2,1,0:T(8,128)} fusion(bf16[2,1024,1024,1]{2,1,0,3:T(8,128)(2,1)S(1)} %bitcast.171, bf16[1,1,2,512,1024]{4,3,2,1,0:T(8,128)(2,1)S(1)} %maximum_bitcast_fusion.4, bf16[1,1,2,512,1024]{4,3,2,1,0:T(8,128)(2,1)S(1)} %fusion.76), kind=kOutput, calls=%fused_computation.11 | convolution fusion | flops 4298113024 | bytes 12582912 | tf_op jit(solution)/shard_map/corit,crjt->coij/dot_general | solution.py:83
  143.5 1.8 fusion.32
  145.3 36.2 %all-gather.5.cloned.1.call-done = bf16[1,2,4,256,1024]{4,3,1,2,0:T(8,128)(2,1)} async-done(((bf16[1,2,4,128,1024]{4,3,1,2,0:T(8,128)(2,1)}), bf16[1,2,4,256,1024]{4,3,1,2,0:T(8,128)(2,1)}) %all-gather.5.cloned.1.call-update) | async-done | bytes 4194320 | tf_op jit(solution)/shard_map/all_gather | solution.py:70
  181.6 4.6 %copy.27 = bf16[1,2,4,256,1024]{4,3,2,1,0:T(8,128)(2,1)} copy(bf16[1,2,4,256,1024]{4,3,1,2,0:T(8,128)(2,1)} %all-gather.5.cloned.1.call-done) | data formatting | bytes 8388608 | tf_op jit(solution)/shard_map/all_gather | solution.py:70
  186.2 42.9 %reduce-scatter.2.cloned.1.call-done = f32[1,2,512,256]{3,2,1,0:T(8,128)} async-done(((f32[1,2,512,1024]{3,2,1,0:T(8,128)}), f32[1,2,512,256]{3,2,1,0:T(8,128)}) %reduce-scatter.2.cloned.1.call-update) | async-done | bytes 1048592 | tf_op jit(solution)/shard_map/reduce_scatter | solution.py:88
  235.6 5.8 %psum.28 = f32[1,2,512]{2,1,0:T(2,128)S(1)} all-reduce(f32[1,2,512]{2,1,0:T(2,128)S(1)} %pad_maximum_fusion), channel_id=1, replica_groups=mesh['freq'=4,'tm'=4,'grp'=2] {'tm'}, use_global_device_ids=true, to_apply=%region_1.3 | all-reduce | flops 1024 | bytes 8192 | tf_op jit(solution)/shard_map/psum | solution.py:98
  241.4 4.4 %all_gather.22 = f32[1,2,1024]{2,1,0:T(2,128)S(1)} all-gather(f32[1,2,512]{2,1,0:T(2,128)S(1)} %fusion.38), channel_id=1, replica_groups=mesh['freq'=4,'tm'=4,'grp'=2] {'grp'}, dimensions={2}, use_global_device_ids=true | all-gather | bytes 12288 | tf_op jit(solution)/shard_map/all_gather | solution.py:101
  248.6 5.7 %psum.29 = f32[1,2,512]{2,1,0:T(2,128)S(1)} all-reduce(f32[1,2,512]{2,1,0:T(2,128)S(1)} %pad_maximum_fusion.1), channel_id=1, replica_groups=mesh['freq'=4,'tm'=4,'grp'=2] {'tm'}, use_global_device_ids=true, to_apply=%region_3.5 | all-reduce | flops 1024 | bytes 8192 | tf_op jit(solution)/shard_map/psum | solution.py:98
  255.0 4.5 %all_gather.23 = f32[1,2,1024]{2,1,0:T(2,128)S(1)} all-gather(f32[1,2,512]{2,1,0:T(2,128)S(1)} %fusion.39), channel_id=1, replica_groups=mesh['freq'=4,'tm'=4,'grp'=2] {'grp'}, dimensions={2}, use_global_device_ids=true | all-gather | bytes 12288 | tf_op jit(solution)/shard_map/all_gather | solution.py:101
  262.4 5.7 %psum.30 = f32[1,2,512]{2,1,0:T(2,128)S(1)} all-reduce(f32[1,2,512]{2,1,0:T(2,128)S(1)} %pad_maximum_fusion.2), channel_id=1, replica_groups=mesh['freq'=4,'tm'=4,'grp'=2] {'tm'}, use_global_device_ids=true, to_apply=%region_5.7 | all-reduce | flops 1024 | bytes 8192 | tf_op jit(solution)/shard_map/psum | solution.py:98
  268.7 4.4 %all_gather.24 = f32[1,2,1024]{2,1,0:T(2,128)S(1)} all-gather(f32[1,2,512]{2,1,0:T(2,128)S(1)} %fusion.40), channel_id=1, replica_groups=mesh['freq'=4,'tm'=4,'grp'=2] {'grp'}, dimensions={2}, use_global_device_ids=true | all-gather | bytes 12288 | tf_op jit(solution)/shard_map/all_gather | solution.py:101
  275.9 5.7 %psum.31 = f32[1,2,512]{2,1,0:T(2,128)S(1)} all-reduce(f32[1,2,512]{2,1,0:T(2,128)S(1)} %pad_maximum_fusion.3), channel_id=1, replica_groups=mesh['freq'=4,'tm'=4,'grp'=2] {'tm'}, use_global_device_ids=true, to_apply=%region_7.9 | all-reduce | flops 1024 | bytes 8192 | tf_op jit(solution)/shard_map/psum | solution.py:98
  282.3 4.4 %all_gather.25 = f32[1,2,1024]{2,1,0:T(2,128)S(1)} all-gather(f32[1,2,512]{2,1,0:T(2,128)S(1)} %fusion.41), channel_id=1, replica_groups=mesh['freq'=4,'tm'=4,'grp'=2] {'grp'}, dimensions={2}, use_global_device_ids=true | all-gather | bytes 12288 | tf_op jit(solution)/shard_map/all_gather | solution.py:101
  286.6 13.4 %all_gather.26 = f32[4,2,1024]{2,1,0:T(2,128)S(1)} all-gather(f32[1,2,1024]{2,1,0:T(2,128)S(1)} %all_gather.25), channel_id=1, replica_groups=mesh['freq'=4,'tm'=4,'grp'=2] {'freq'}, dimensions={0}, use_global_device_ids=true | all-gather | bytes 40960 | tf_op jit(solution)/shard_map/all_gather | solution.py:102
  302.1 4.6 %fusion.8 = bf16[1,2,2,128,1024]{4,3,2,1,0:T(8,128)(2,1)} fusion(bf16[2,1,128,2,512]{4,2,3,1,0:T(8,128)(2,1)S(1)} %get-tuple-element.17, bf16[2,1,128,2,512]{4,2,3,1,0:T(8,128)(2,1)S(1)} %get-tuple-element.16, bf16[2,2,512,1024]{3,2,1,0:T(8,128)(2,1)} %bitcast.170, bf16[2,512]{1,0:T(2,128)(2,1)S(1)} %convert_element_type.50), kind=kOutput, calls=%fused_computation.19 | convolution fusion | flops 1076887552 | bytes 6293504 | tf_op jit(solution)/shard_map/cpobrq,crpqt->cpobt/dot_general | solution.py:114
  (95 shorter events, 25.7 us)
Async XLA Ops:
  7.2 1.6 copy-start
  7.2 118.9 %all-gather.3.cloned.1.call-start = ((), (), s32[]{:S(2)}) async-start(), calls=%async_computation.3 | async-start | bytes 6291456 | tf_op jit(solution)/shard_map/all_gather | solution.py:69
  67.2 114.4 %all-gather.5.cloned.1.call-start = ((), (), s32[]{:S(2)}) async-start(), calls=%async_computation.5 | async-start | bytes 6291456 | tf_op jit(solution)/shard_map/all_gather | solution.py:70
  121.8 0.7 copy-start.5
  121.8 0.7 copy-start.1
  121.8 107.3 %reduce-scatter.2.cloned.1.call-start = ((), (), s32[]{:S(2)}) async-start(), calls=%async_computation.4 | async-start | bytes 5242880 | tf_op jit(solution)/shard_map/reduce_scatter | solution.py:88
  128.7 2.3 copy-start.3
  138.7 0.7 copy-start.8
  138.7 1.3 copy-start.7
  138.7 3.1 copy-start.4
  138.7 4.3 %copy-start.9 = (s32[2,256]{1,0:T(2,128)S(1)}, s32[2,256]{1,0:T(2,128)}, u32[]{:S(2)}) copy-start(s32[2,256]{1,0:T(2,128)} %param.15) | copy-start | bytes 6148
  229.1 17.3 %copy-start.2 = (f32[1,2,512,256]{3,2,1,0:T(8,128)S(1)}, f32[1,2,512,256]{3,2,1,0:T(8,128)}, u32[]{:S(2)}) copy-start(f32[1,2,512,256]{3,2,1,0:T(8,128)} %reduce-scatter.2.cloned.1.call-done) | copy-start | bytes 3145732
  260.1 39.9 %copy-start.6 = (s32[4]{0:T(128)S(1)}, s32[4]{0:T(128)}, u32[]{:S(2)}) copy-start(s32[4]{0:T(128)} %param.16) | copy-start | bytes 52
Sparse Core Ops, SparseCore 0:
  67.3 55.9 all-gather.2
  124.8 56.7 all-gather.4
  184.7 44.3 reduce-scatter.1
where the time goes:
time: 315 us; the launch traced here: 314 us
  blocking collectives  159 us (50%)
  waiting for transfers between devices  79.2 us (25%)
  matrix products  24.5 us (8%)
  local copies, waits for them, and re-layouts  19 us (6%)
  between operations  17.3 us (5%)
  other arithmetic  14.7 us (5%)
    all_to_all x1, blocking collectives, body(): lax.all_to_all(corr_source, 'freq', split_axis=0, concat_axis=2, tiled=True)  54.4 us
    all_to_all x1, blocking collectives, body(): lax.all_to_all(beam_source, 'freq', split_axis=0, concat_axis=2, tiled=True)  50.7 us
    reduce_scatter x1, waiting for transfers between devices, body(): lax.psum_scatter(partial_value, 'tm', scatter_dimension=3, tiled=True)  42.9 us
    all_gather x1, waiting for transfers between devices, body(): lax.all_gather(beam_half.reshape(split_shape), 'grp', axis=3, tiled=True)  36.2 us
    psum x4, blocking collectives, body(): update = lax.psum(update, 'tm')  22.8 us
    all_gather x4, blocking collectives, body(): gains = lax.all_gather(fresh, 'grp', axis=2, tiled=True)  17.6 us
    all_gather x1, blocking collectives, body(): all_gains = lax.all_gather(gains, 'freq', axis=0, tiled=True)  13.4 us
  transfers between devices with their start and end apart: 3, of which 2 were waited for; matrix products, arithmetic and copies ran while one was open for 9% of the time, Pallas kernels for 0%

commit v1 on v0

--- a/solution.py
+++ b/solution.py
@@ -62,7 +62,15 @@
     beam_source = jnp.take(voltages, beam_channels, axis=0)
     corr_half, beam_half = (
         lax.all_to_all(corr_source, "freq", split_axis=0, concat_axis=2, tiled=True),
-        lax.all_to_all(beam_source, "freq", split_axis=0, concat_axis=2, tiled=True),
+        jnp.concatenate(
+            lax.all_to_all(
+                jnp.stack(jnp.split(beam_source, lax.psum(1, axis_name="freq"), axis=0), axis=0),
+                axis_name="freq",
+                split_axis=0,
+                concat_axis=0,
+            ),
+            2,
+        ),
     )
     split_shape = (per_device, 2, n_freq, per_input, samples)
     corr_pair, beam_pair = (

time: 315 us -> 285 us (0.905)
  blocking collectives: 159 us -> 110 us
  waiting for transfers between devices: 79.2 us -> 94.1 us
  starting transfers between devices: 0.12 us -> 4.86 us
    all_gather x1, waiting for transfers between devices: 0.01 us -> 51.8 us  [body(): lax.all_gather(corr_half.reshape(split_shape), 'grp', axis=3, tiled=True)]
    all_to_all x1 -> x0, blocking collectives: 50.7 us -> none  [body(): lax.all_to_all(beam_source, 'freq', split_axis=0, concat_axis=2, tiled=True)]
    reduce_scatter x1, waiting for transfers between devices: 42.9 us -> 0.02 us  [body(): lax.psum_scatter(partial_value, 'tm', scatter_dimension=3, tiled=True)]
    all_to_all x0 -> x1, waiting for transfers between devices: none -> 42.2 us  [body(): lax.all_to_all(jnp.stack(jnp.split(beam_source, lax.psum(1, axis_name='fr...]
    all_gather x1, waiting for transfers between devices: 36.2 us -> 0.02 us  [body(): lax.all_gather(beam_half.reshape(split_shape), 'grp', axis=3, tiled=True)]
    all_to_all x0 -> x1, starting transfers between devices: none -> 4.77 us  [body(): lax.all_to_all(jnp.stack(jnp.split(beam_source, lax.psum(1, axis_name='fr...]
    all_gather x1 -> x0, local copies, waits for them, and re-layouts: 4.6 us -> none  [body(): lax.all_gather(beam_half.reshape(split_shape), 'grp', axis=3, tiled=True)]
    all_to_all x0 -> x1, local copies, waits for them, and re-layouts: none -> 3.15 us  [body(): lax.all_to_all(jnp.stack(jnp.split(beam_source, lax.psum(1, axis_name='fr...]
  transfers between devices with their start and end apart: 3 -> 4, of which waited for: 2 -> 2; matrix products, arithmetic and copies ran while one was open for 9% -> 12% of each run, Pallas kernels for 0% -> 0%
where the time goes in v1:
time: 285 us; the launch traced here: 284 us
  blocking collectives  110 us (39%)
  waiting for transfers between devices  94.1 us (33%)
  matrix products  24.7 us (9%)
  local copies, waits for them, and re-layouts  19.3 us (7%)
  between operations  17.4 us (6%)
  other arithmetic  14.1 us (5%)
  starting transfers between devices  4.86 us (2%)
    all_to_all x1, blocking collectives, body(): lax.all_to_all(corr_source, 'freq', split_axis=0, concat_axis=2, tiled=True)  54.4 us
    all_gather x1, waiting for transfers between devices, body(): lax.all_gather(corr_half.reshape(split_shape), 'grp', axis=3, tiled=True)  51.8 us
    all_to_all x1, waiting for transfers between devices, body(): lax.all_to_all(jnp.stack(jnp.split(beam_source, lax.psum(1, axis_name='fr...  42.2 us
    psum x4, blocking collectives, body(): update = lax.psum(update, 'tm')  23.9 us
    all_gather x4, blocking collectives, body(): gains = lax.all_gather(fresh, 'grp', axis=2, tiled=True)  18.2 us
    all_gather x1, blocking collectives, body(): all_gains = lax.all_gather(gains, 'freq', axis=0, tiled=True)  13.1 us
    dot_general x1, matrix products, body(): jnp.einsum('corit,crjt->coij', left, corr_volts, preferred_element_type=j...  6.11 us
  transfers between devices with their start and end apart: 4, of which 2 were waited for; matrix products, arithmetic and copies ran while one was open for 12% of the time, Pallas kernels for 0%

profile of v1, /device:TPU:0, one launch (start us, length us, event | category | flops | bytes accessed | tf_op | source)
XLA Modules:
  0.0 284.2 jit_solution(13020526652034354769)
XLA Ops:
  8.8 2.0 gather_fusion.2
  10.8 1.9 broadcast_select_fusion.1
  12.7 54.4 %all_to_all.20 = bf16[4,2,128,1024]{3,2,1,0:T(8,128)(2,1)} all-to-all(bf16[4,2,128,1024]{3,2,1,0:T(8,128)(2,1)S(1)} %broadcast_select_fusion.1), channel_id=1, replica_groups=mesh['freq'=4,'tm'=4,'grp'=2] {'freq'}, dimensions={0} | all-to-all | bytes 4194304 | tf_op jit(solution)/shard_map/all_to_all | solution.py:64
  67.8 3.5 %gather_fusion = s32[512]{0:T(512)S(1)} fusion(s32[512]{0:T(512)S(1)} %copy-done.1, s32[1024]{0:T(1024)S(1)} %pad_clamp_fusion.1), kind=kCustom, calls=%fused_computation.2 | custom fusion | bytes 6144 | tf_op jit(solution)/shard_map/jit(_take)/gather | solution.py:83
  71.5 51.8 %all-gather.3.cloned.1.call-done = bf16[1,2,4,256,1024]{4,3,1,2,0:T(8,128)(2,1)} async-done(((bf16[1,2,4,128,1024]{4,3,1,2,0:T(8,128)(2,1)}), bf16[1,2,4,256,1024]{4,3,1,2,0:T(8,128)(2,1)}) %all-gather.3.cloned.1.call-update) | async-done | bytes 4194320 | tf_op jit(solution)/shard_map/all_gather | solution.py:77
  123.3 2.6 copy.28
  126.7 1.8 copy-done.3
  129.7 6.1 %fusion.5 = f32[1,2,512,1024]{3,2,1,0:T(8,128)} fusion(bf16[2,1024,1024,1]{2,1,0,3:T(8,128)(2,1)S(1)} %bitcast.178, bf16[1,1,2,512,1024]{4,3,2,1,0:T(8,128)(2,1)S(1)} %maximum_bitcast_fusion.4, bf16[1,1,2,512,1024]{4,3,2,1,0:T(8,128)(2,1)S(1)} %fusion.76), kind=kOutput, calls=%fused_computation.11 | convolution fusion | flops 4298113024 | bytes 12582912 | tf_op jit(solution)/shard_map/corit,crjt->coij/dot_general | solution.py:91
  135.8 2.0 gather_fusion.3
  137.8 1.9 broadcast_select_fusion
  141.5 4.8 %all-to-all-start.1 = ((bf16[4,1,2,128,1024]{4,3,2,1,0:T(8,128)(2,1)}), bf16[4,1,2,128,1024]{4,3,2,1,0:T(8,128)(2,1)}, u32[]{:S(2)}, u32[]{:S(2)}) async-start(bf16[4,1,2,128,1024]{4,3,2,1,0:T(8,128)(2,1)} %pad_maximum_fusion), calls=%async_computation.2 | async-start | bytes 4194304 | tf_op jit(solution)/shard_map/all_to_all | solution.py:66
  150.6 1.8 fusion.32
  152.4 42.2 %all-to-all-done.1 = bf16[4,1,2,128,1024]{4,3,2,1,0:T(8,128)(2,1)} async-done(((bf16[4,1,2,128,1024]{4,3,2,1,0:T(8,128)(2,1)}), bf16[4,1,2,128,1024]{4,3,2,1,0:T(8,128)(2,1)}, u32[]{:S(2)}, u32[]{:S(2)}) %all-to-all-start.1) | async-done | bytes 2097184 | tf_op jit(solution)/shard_map/all_to_all | solution.py:66
  194.6 3.2 %copy.52 = bf16[4,1,2,128,1024]{4,3,0,2,1:T(8,128)(2,1)} copy(bf16[4,1,2,128,1024]{4,3,2,1,0:T(8,128)(2,1)} %all-to-all-done.1) | data formatting | bytes 4194304 | tf_op jit(solution)/shard_map/all_to_all | solution.py:66
  204.5 5.7 %psum.28 = f32[1,2,512]{2,1,0:T(2,128)S(1)} all-reduce(f32[1,2,512]{2,1,0:T(2,128)S(1)} %pad_maximum_fusion.1), channel_id=1, replica_groups=mesh['freq'=4,'tm'=4,'grp'=2] {'tm'}, use_global_device_ids=true, to_apply=%region_1.3 | all-reduce | flops 1024 | bytes 8192 | tf_op jit(solution)/shard_map/psum | solution.py:106
  210.1 4.6 %all_gather.22 = f32[1,2,1024]{2,1,0:T(2,128)S(1)} all-gather(f32[1,2,512]{2,1,0:T(2,128)S(1)} %fusion.38), channel_id=1, replica_groups=mesh['freq'=4,'tm'=4,'grp'=2] {'grp'}, dimensions={2}, use_global_device_ids=true | all-gather | bytes 12288 | tf_op jit(solution)/shard_map/all_gather | solution.py:109
  218.2 6.1 %psum.29 = f32[1,2,512]{2,1,0:T(2,128)S(1)} all-reduce(f32[1,2,512]{2,1,0:T(2,128)S(1)} %pad_maximum_fusion.2), channel_id=1, replica_groups=mesh['freq'=4,'tm'=4,'grp'=2] {'tm'}, use_global_device_ids=true, to_apply=%region_3.5 | all-reduce | flops 1024 | bytes 8192 | tf_op jit(solution)/shard_map/psum | solution.py:106
  224.3 4.8 %all_gather.23 = f32[1,2,1024]{2,1,0:T(2,128)S(1)} all-gather(f32[1,2,512]{2,1,0:T(2,128)S(1)} %fusion.39), channel_id=1, replica_groups=mesh['freq'=4,'tm'=4,'grp'=2] {'grp'}, dimensions={2}, use_global_device_ids=true | all-gather | bytes 12288 | tf_op jit(solution)/shard_map/all_gather | solution.py:109
  232.6 6.1 %psum.30 = f32[1,2,512]{2,1,0:T(2,128)S(1)} all-reduce(f32[1,2,512]{2,1,0:T(2,128)S(1)} %pad_maximum_fusion.3), channel_id=1, replica_groups=mesh['freq'=4,'tm'=4,'grp'=2] {'tm'}, use_global_device_ids=true, to_apply=%region_5.7 | all-reduce | flops 1024 | bytes 8192 | tf_op jit(solution)/shard_map/psum | solution.py:106
  238.7 4.6 %all_gather.24 = f32[1,2,1024]{2,1,0:T(2,128)S(1)} all-gather(f32[1,2,512]{2,1,0:T(2,128)S(1)} %fusion.40), channel_id=1, replica_groups=mesh['freq'=4,'tm'=4,'grp'=2] {'grp'}, dimensions={2}, use_global_device_ids=true | all-gather | bytes 12288 | tf_op jit(solution)/shard_map/all_gather | solution.py:109
  246.8 6.1 %psum.31 = f32[1,2,512]{2,1,0:T(2,128)S(1)} all-reduce(f32[1,2,512]{2,1,0:T(2,128)S(1)} %pad_maximum_fusion.4), channel_id=1, replica_groups=mesh['freq'=4,'tm'=4,'grp'=2] {'tm'}, use_global_device_ids=true, to_apply=%region_7.9 | all-reduce | flops 1024 | bytes 8192 | tf_op jit(solution)/shard_map/psum | solution.py:106
  252.8 4.4 %all_gather.25 = f32[1,2,1024]{2,1,0:T(2,128)S(1)} all-gather(f32[1,2,512]{2,1,0:T(2,128)S(1)} %fusion.41), channel_id=1, replica_groups=mesh['freq'=4,'tm'=4,'grp'=2] {'grp'}, dimensions={2}, use_global_device_ids=true | all-gather | bytes 12288 | tf_op jit(solution)/shard_map/all_gather | solution.py:109
  257.2 13.1 %all_gather.26 = f32[4,2,1024]{2,1,0:T(2,128)S(1)} all-gather(f32[1,2,1024]{2,1,0:T(2,128)S(1)} %all_gather.25), channel_id=1, replica_groups=mesh['freq'=4,'tm'=4,'grp'=2] {'freq'}, dimensions={0}, use_global_device_ids=true | all-gather | bytes 40960 | tf_op jit(solution)/shard_map/all_gather | solution.py:110
  272.5 4.5 %fusion.8 = bf16[1,2,2,128,1024]{4,3,2,1,0:T(8,128)(2,1)} fusion(bf16[2,1,128,2,512]{4,2,3,1,0:T(8,128)(2,1)S(1)} %get-tuple-element.21, bf16[2,1,128,2,512]{4,2,3,1,0:T(8,128)(2,1)S(1)} %get-tuple-element.20, bf16[2,2,512,1024]{3,2,1,0:T(8,128)(2,1)} %bitcast.204, bf16[2,512]{1,0:T(2,128)(2,1)S(1)} %convert_element_type.50), kind=kOutput, calls=%fused_computation.21 | convolution fusion | flops 1076887552 | bytes 6293504 | tf_op jit(solution)/shard_map/cpobrq,crpqt->cpobt/dot_general | solution.py:122
  (98 shorter events, 27.1 us)
Async XLA Ops:
  7.2 1.6 copy-start
  7.2 116.1 %all-gather.3.cloned.1.call-start = ((), (), s32[]{:S(2)}) async-start(), calls=%async_computation.3 | async-start | bytes 6291456 | tf_op jit(solution)/shard_map/all_gather | solution.py:77
  67.1 0.7 copy-start.5
  67.1 0.7 copy-start.1
  67.2 130.6 %reduce-scatter.2.cloned.1.call-start = ((), (), s32[]{:S(2)}) async-start(), calls=%async_computation.4 | async-start | bytes 5242880 | tf_op jit(solution)/shard_map/reduce_scatter | solution.py:96
  126.3 2.2 copy-start.3
  141.5 4.8 %copy-start.8 = (s32[4]{0:T(128)S(1)}, s32[4]{0:T(128)}, u32[]{:S(2)}) copy-start(s32[4]{0:T(128)} %param.17) | copy-start | bytes 52
  141.5 5.5 %copy-start.7 = (f32[2,512]{1,0:T(2,128)S(1)}, f32[2,512]{1,0:T(2,128)}, u32[]{:S(2)}) copy-start(f32[2,512]{1,0:T(2,128)} %param.14) | copy-start | bytes 12292
  141.5 7.3 %copy-start.4 = (f32[1,2,1024]{2,1,0:T(2,128)S(1)}, f32[1,2,1024]{2,1,0:T(2,128)}, u32[]{:S(2)}) copy-start(f32[1,2,1024]{2,1,0:T(2,128)} %param.11) | copy-start | bytes 24580
  141.5 8.6 %copy-start.9 = (s32[2,256]{1,0:T(2,128)S(1)}, s32[2,256]{1,0:T(2,128)}, u32[]{:S(2)}) copy-start(s32[2,256]{1,0:T(2,128)} %param.15) | copy-start | bytes 6148
  141.5 53.1 %all-to-all-start.1 = ((bf16[4,1,2,128,1024]{4,3,2,1,0:T(8,128)(2,1)}), bf16[4,1,2,128,1024]{4,3,2,1,0:T(8,128)(2,1)}, u32[]{:S(2)}, u32[]{:S(2)}) async-start(bf16[4,1,2,128,1024]{4,3,2,1,0:T(8,128)(2,1)} %pad_maximum_fusion), calls=%async_computation.2 | async-start | bytes 4194304 | tf_op jit(solution)/shard_map/all_to_all | solution.py:66
  146.2 126.3 %all-gather.5.cloned.1.call-start = ((), (), s32[]{:S(2)}) async-start(), calls=%async_computation.5 | async-start | bytes 6291456 | tf_op jit(solution)/shard_map/all_gather | solution.py:78
  197.8 16.9 %copy-start.2 = (f32[1,2,512,256]{3,2,1,0:T(8,128)S(1)}, f32[1,2,512,256]{3,2,1,0:T(8,128)}, u32[]{:S(2)}) copy-start(f32[1,2,512,256]{3,2,1,0:T(8,128)} %reduce-scatter.2.cloned.1.call-done) | copy-start | bytes 3145732
  230.3 40.0 %copy-start.6 = (s32[4]{0:T(128)S(1)}, s32[4]{0:T(128)}, u32[]{:S(2)}) copy-start(s32[4]{0:T(128)} %param.16) | copy-start | bytes 52
Sparse Core Ops, SparseCore 0:
  67.3 55.9 all-gather.2
  135.9 44.3 reduce-scatter.1
  197.9 54.9 all-gather.4
